TPU v7x, 128 devices: a whole 4x4x4 slice. The times are simulated.
128 devices in a mesh: req: 32 (over x, z, core), tp: 4 (over y).
Axes of the slice: x: 4, y: 4, z: 4, core: 2. Of those that a mesh axis runs over, the one named last changes fastest.
Arguments:
- tokens: bfloat16 [65536, 1024], P('req'), may hold values from -6 to 6
- attn_gain: bfloat16 [1024], replicated, may hold values from 0.5 to 1.5
- w_query: bfloat16 [1024, 1024], P(None, 'tp'), may hold values from -1 to 1
- w_key: bfloat16 [1024, 1024], P(None, 'tp'), may hold values from -1 to 1
- w_value: bfloat16 [1024, 1024], P(None, 'tp'), may hold values from -0.1875 to 0.1875
- persist_key: bfloat16 [16, 1024], P(None, 'tp'), may hold values from -250 to 250
- persist_value: bfloat16 [16, 1024], P(None, 'tp'), may hold values from -6 to 6
- log_forget: float32 [65536, 8], P('req', 'tp'), may hold values from -0.75 to 0
- mem_gain: float32 [1024], P('tp'), may hold values from 0.5 to 1.5
- w_out: bfloat16 [1024, 1024], P('tp'), may hold values from -0.1875 to 0.1875
- ffn_gain: bfloat16 [1024], replicated, may hold values from 0.5 to 1.5
- w_gate: bfloat16 [1024, 2816], P(None, 'tp'), may hold values from -0.1875 to 0.1875
- w_up: bfloat16 [1024, 2816], P(None, 'tp'), may hold values from -0.1875 to 0.1875
- w_down: bfloat16 [2816, 1024], P('tp'), may hold values from -0.109375 to 0.109375
- doc_ids: int32 [65536], P('req'), may hold values from 0 to 512, never falling along the last dimension, each value on 1 to 32768 neighbouring positions
- page_owner: int32 [512], P('req'), may hold values from 0 to 31, as said below
- page_slot: int32 [512], P('req'), may hold values from 0 to 15
Outputs:
- layer_out: bfloat16 [65536, 1024], P('req')
- kv_cache: bfloat16 [512, 128, 2048], P('req', None, 'tp')
Inputs may be any that keep to these rules, and one draw needn't show every extreme that they name: `page_owner`: the pages of one index of req going to one owner number at most 1, and every owner receives exactly 16 pages, one for each of its slots.
All inputs are finite; a program needn't handle non-finite values.
Results may differ from a plain program's by a relative error of at most 0.015.
Values may be sent and summed in bfloat16 or wider, within the bound.
No kernel may reach another device: no remote copies, remote signals or barrier semaphores. Data moves between devices by JAX's collectives and lax.ppermute only.
A program may use at most 128 MiB of HBM per device.

v0:
```python
import math
import jax
import jax.numpy as jnp
from jax import lax
from jax.sharding import PartitionSpec as P

HEAD_DIM = 128
PERSIST = 16
SEG = 1024
PAGE = 128
norm_eps = 1e-05
unit_eps = 1e-06
big_negative = -1e30


def entering(shard, axis, combine, identity):
    devices, position = (lax.axis_size(axis), lax.axis_index(axis))
    everything = jax.tree.map(lambda part: lax.all_gather(part, axis), shard)
    start = jax.tree.map(
        lambda part, zero: jnp.broadcast_to(jnp.asarray(zero, part.dtype), part.shape),
        shard,
        identity,
    )

    def step(k, before):
        reached = k < position
        new = combine(before, jax.tree.map(lambda part: part[k], everything))
        return jax.tree.map(lambda a, b: jnp.where(reached, a, b), new, before)

    return lax.fori_loop(0, devices, step, start)


def rms_scale(values, gain):
    wide = values.astype(jnp.float32)
    return (
        wide
        * lax.rsqrt(jnp.mean(wide * wide, axis=-1, keepdims=True) + norm_eps)
        * gain.astype(jnp.float32)
    )


def unit_rows(values):
    wide = values.astype(jnp.float32)
    return (
        wide
        * lax.rsqrt(jnp.mean(wide * wide, axis=-1, keepdims=True) + unit_eps)
        / math.sqrt(wide.shape[-1])
    )


def attend(queries, key_rows, value_rows, docs, persist_keys, persist_values):
    scale = 1.0 / math.sqrt(queries.shape[-1])
    local = (
        jnp.einsum("thd,shd->hts", queries, key_rows, preferred_element_type=jnp.float32) * scale
    )
    order = jnp.arange(docs.shape[0])
    allowed = (order[None, :] <= order[:, None]) & (docs[None, :] == docs[:, None])
    local = jnp.where(allowed[None], local, big_negative)
    persist = (
        jnp.einsum("thd,phd->htp", queries, persist_keys, preferred_element_type=jnp.float32)
        * scale
    )
    peak = jnp.maximum(jnp.max(persist, axis=-1), jnp.max(local, axis=-1))
    weight_persist = jnp.exp(persist - peak[..., None])
    weight_local = jnp.exp(local - peak[..., None])
    total = jnp.sum(weight_persist, axis=-1) + jnp.sum(weight_local, axis=-1)
    probs_persist = (weight_persist / total[..., None]).astype(jnp.bfloat16)
    probs_local = (weight_local / total[..., None]).astype(jnp.bfloat16)
    return jnp.einsum(
        "htp,phd->thd", probs_persist, persist_values, preferred_element_type=jnp.float32
    ) + jnp.einsum("hts,shd->thd", probs_local, value_rows, preferred_element_type=jnp.float32)


def memory_block(carry, inputs):
    state, carried = carry
    q_unit, k_unit, value_rows, decay_log, docs = inputs
    value_wide = value_rows.astype(jnp.float32)
    cumul = jnp.cumsum(decay_log, axis=0)
    diff = cumul[:, None, :] - cumul[None, :, :]
    order = jnp.arange(docs.shape[0])
    allowed = ((order[None, :] <= order[:, None]) & (docs[None, :] == docs[:, None]))[:, :, None]
    decay = jnp.where(allowed, jnp.exp(jnp.where(allowed, diff, 0.0)), 0.0)
    inner = jnp.einsum("thd,shd->tsh", q_unit, k_unit, precision=lax.Precision.HIGHEST) * decay
    recall = jnp.einsum("tsh,shd->thd", inner, value_wide, precision=lax.Precision.HIGHEST)
    continues = (docs == carried).astype(jnp.float32)
    reach = jnp.exp(cumul) * continues[:, None]
    recall = (
        recall
        + jnp.einsum("thd,hde->the", q_unit, state, precision=lax.Precision.HIGHEST)
        * reach[:, :, None]
    )
    last_doc = docs[-1]
    keep = jnp.exp(cumul[-1][None, :] - cumul) * (docs == last_doc).astype(jnp.float32)[:, None]
    kept = jnp.exp(cumul[-1]) * (last_doc == carried).astype(jnp.float32)
    state_next = (
        jnp.einsum(
            "shd,she->hde", k_unit * keep[:, :, None], value_wide, precision=lax.Precision.HIGHEST
        )
        + state * kept[:, None, None]
    )
    return ((state_next, last_doc), recall)


def combine_maps(earlier, later):
    joins = jnp.logical_or(
        jnp.logical_or(earlier[3] == later[2], earlier[3] < 0), later[2] < 0
    ).astype(jnp.float32)
    carry_factor = later[0] * joins
    return (
        carry_factor * earlier[0],
        carry_factor[:, None, None] * earlier[1] + later[1],
        jnp.where(earlier[2] < 0, later[2], earlier[2]),
        jnp.where(later[3] < 0, earlier[3], later[3]),
    )


def place_pages(key3, value3, page_owner, page_slot):
    page_count = page_owner.shape[0]
    req_count = lax.axis_size("req")
    capacity = max(1, page_count // req_count)
    pages = jnp.stack([key3, value3], axis=2).reshape(page_count, -1)
    order = jnp.arange(page_count)
    same_owner = page_owner[:, None] == page_owner[None, :]
    rank = jnp.sum((same_owner & (order[:, None] < order[None, :])).astype(jnp.int32), axis=0)
    bucket = page_owner * capacity + rank
    targets = jnp.arange(req_count * capacity)
    routing = targets[:, None] == bucket[None, :]
    outgoing = jnp.dot(
        routing.astype(jnp.bfloat16), pages, preferred_element_type=jnp.float32
    ).astype(jnp.bfloat16)
    outgoing = outgoing.reshape(req_count, capacity, -1)
    codes = (jnp.sum(routing.astype(jnp.int32) * (page_slot[None, :] + 1), axis=1) - 1).astype(
        jnp.bfloat16
    )
    codes = codes.reshape(req_count, capacity)
    arrived, arrived_codes = (
        lax.all_to_all(outgoing, "req", split_axis=0, concat_axis=0, tiled=True),
        lax.all_to_all(codes, "req", split_axis=0, concat_axis=0, tiled=True),
    )
    wanted = (
        arrived_codes.reshape(-1).astype(jnp.float32)[None, :]
        == jnp.arange(page_count).astype(jnp.float32)[:, None]
    )
    cache = jnp.dot(
        wanted.astype(jnp.bfloat16),
        arrived.reshape(req_count * capacity, -1),
        preferred_element_type=jnp.float32,
    )
    return cache.astype(jnp.bfloat16).reshape(page_count, PAGE, -1)


def on_device(
    tokens,
    attn_gain,
    w_query,
    w_key,
    w_value,
    persist_key,
    persist_value,
    log_forget,
    mem_gain,
    w_out,
    ffn_gain,
    w_gate,
    w_up,
    w_down,
    doc_ids,
    page_owner,
    page_slot,
):
    tok_count = tokens.shape[0]
    heads_here = w_query.shape[1] // HEAD_DIM
    normed = rms_scale(tokens, attn_gain).astype(jnp.bfloat16)
    queries = jnp.dot(normed, w_query, preferred_element_type=jnp.float32).astype(jnp.bfloat16)
    key_rows = jnp.dot(normed, w_key, preferred_element_type=jnp.float32).astype(jnp.bfloat16)
    value_rows = jnp.dot(normed, w_value, preferred_element_type=jnp.float32).astype(jnp.bfloat16)
    shape3 = (tok_count, heads_here, HEAD_DIM)
    kv_cache = place_pages(
        key_rows.reshape(shape3), value_rows.reshape(shape3), page_owner, page_slot
    )
    blocks = tok_count // SEG
    shape4 = (blocks, SEG, heads_here, HEAD_DIM)
    q_unit = unit_rows(queries.reshape(shape3))
    k_unit = unit_rows(key_rows.reshape(shape3))
    doc_blocks = doc_ids.reshape(blocks, SEG)
    mem_rows = math.gcd(tok_count, 512)
    mem_blocks = tok_count // mem_rows
    mem_shape = (mem_blocks, mem_rows, heads_here, HEAD_DIM)
    start = (jnp.zeros((heads_here, HEAD_DIM, HEAD_DIM), jnp.float32), jnp.int32(-1))
    finish, recall = lax.scan(
        memory_block,
        start,
        (
            q_unit.reshape(mem_shape),
            k_unit.reshape(mem_shape),
            value_rows.reshape(mem_shape),
            log_forget.reshape(mem_blocks, mem_rows, heads_here),
            doc_ids.reshape(mem_blocks, mem_rows),
        ),
    )
    local_state = finish[0]
    recall = recall.reshape(shape3)
    cumul = jnp.cumsum(log_forget, axis=0)
    whole_doc = (doc_ids[0] == doc_ids[-1]).astype(jnp.float32)
    element = (
        jnp.exp(cumul[-1]) * whole_doc,
        local_state,
        doc_ids[0].astype(jnp.float32),
        doc_ids[-1].astype(jnp.float32),
    )
    identity = (
        jnp.ones((heads_here,), jnp.float32),
        jnp.zeros_like(local_state),
        jnp.float32(-1.0),
        jnp.float32(-1.0),
    )
    prefix = entering(element, "req", combine_maps, identity)
    continues = (doc_ids.astype(jnp.float32) == prefix[3]).astype(jnp.float32)
    reach = jnp.exp(cumul) * continues[:, None]
    recall = (
        recall
        + jnp.einsum("thd,hde->the", q_unit, prefix[1], precision=lax.Precision.HIGHEST)
        * reach[:, :, None]
    )
    persist_keys = persist_key.reshape(PERSIST, heads_here, HEAD_DIM)
    persist_values = persist_value.reshape(PERSIST, heads_here, HEAD_DIM)

    def attend_block(parts):
        return attend(parts[0], parts[1], parts[2], parts[3], persist_keys, persist_values)

    attended = lax.map(
        attend_block,
        (queries.reshape(shape4), key_rows.reshape(shape4), value_rows.reshape(shape4), doc_blocks),
    )
    memory_out = rms_scale(recall, mem_gain.reshape(heads_here, HEAD_DIM))
    heads_out = (
        (attended.reshape(shape3) + memory_out)
        .astype(jnp.bfloat16)
        .reshape(tok_count, heads_here * HEAD_DIM)
    )
    head_total = lax.psum(jnp.dot(heads_out, w_out, preferred_element_type=jnp.float32), "tp")
    resid = (tokens.astype(jnp.float32) + head_total).astype(jnp.bfloat16)
    normed_ffn = rms_scale(resid, ffn_gain).astype(jnp.bfloat16)
    gate_proj = jnp.dot(normed_ffn, w_gate, preferred_element_type=jnp.float32)
    up_proj = jnp.dot(normed_ffn, w_up, preferred_element_type=jnp.float32)
    hidden = (jax.nn.silu(gate_proj) * up_proj).astype(jnp.bfloat16)
    unit_total = lax.psum(
        jnp.dot(hidden, w_down, preferred_element_type=jnp.float32).astype(jnp.bfloat16), "tp"
    ).astype(jnp.float32)
    layer_out = (resid.astype(jnp.float32) + unit_total).astype(jnp.bfloat16)
    return (layer_out, kv_cache)


def solution(mesh):
    return jax.shard_map(
        on_device,
        mesh=mesh,
        in_specs=(
            P("req", None),
            P(),
            P(None, "tp"),
            P(None, "tp"),
            P(None, "tp"),
            P(None, "tp"),
            P(None, "tp"),
            P("req", "tp"),
            P("tp"),
            P("tp", None),
            P(),
            P(None, "tp"),
            P(None, "tp"),
            P("tp", None),
            P("req"),
            P("req"),
            P("req"),
        ),
        out_specs=(P("req", None), P("req", None, "tp")),
        check_vma=False,
    )
```

profile of v0, /device:TPU:1, one launch (start us, length us, event | category | flops | bytes accessed | tf_op | source)
XLA Modules:
  0.0 916.4 jit_solution(10726321676844413340)
XLA Ops:
  8.1 3.4 fusion.62
  11.5 3.6 multiply_reduce_fusion.1
  36.0 4.2 multiply_multiply_fusion
  40.2 113.1 %while.42 = (s32[]{:T(128)}, f32[2,128,128]{2,1,0:T(8,128)}, s32[]{:T(128)}, f32[4,512,2,128]{1,0,3,2:T(4,128)}, f32[4,512,2,128]{3,1,2,0:T(8,128)}, /*index=5*/...) while((s32[]{:T(128)}, f32[2,128,128]{2,1,0:T(8,128)}, ...), condition=%wide.region_12.13_spmd.clone, body=%wide.region_9.12_spmd.clone.sunk | while | flops 2016809984 | bytes 11492285 | solution.py:190
  40.3 3.0 fusion.150
  46.0 3.3 fusion.152
  56.8 11.1 %dynamic_update_slice.12 = f32[4,512,2,128]{1,0,3,2:T(4,128)} dynamic-update-slice(f32[4,512,2,128]{1,0,3,2:T(4,128)} %get-tuple-element.758, f32[1,512,2,128]{1,0,3,2:T(1,128)S(1)} %copy.278, s32[]{:T(128)S(6)} %copy.291, s32[]{:T(128)} %constant.104.clone.1..sunk.1, s32[]{:T(128)} %constant.104.clone.1..sunk.1, s32[]{:T(128)} %constant.104.clone.1..sunk.1) | dynamic-update-slice | bytes 1048580 | tf_op jit(solution)/shard_map/while/body/jit(dynamic_update_index_in_dim)/dynamic_update_slice | solution.py:190
  68.5 3.0 fusion.150
  74.2 3.3 fusion.152
  85.1 11.1 %dynamic_update_slice.12 = f32[4,512,2,128]{1,0,3,2:T(4,128)} dynamic-update-slice(f32[4,512,2,128]{1,0,3,2:T(4,128)} %get-tuple-element.758, f32[1,512,2,128]{1,0,3,2:T(1,128)S(1)} %copy.278, s32[]{:T(128)S(6)} %copy.291, s32[]{:T(128)} %constant.104.clone.1..sunk.1, s32[]{:T(128)} %constant.104.clone.1..sunk.1, s32[]{:T(128)} %constant.104.clone.1..sunk.1) | dynamic-update-slice | bytes 1048580 | tf_op jit(solution)/shard_map/while/body/jit(dynamic_update_index_in_dim)/dynamic_update_slice | solution.py:190
  102.5 3.3 fusion.152
  113.4 11.1 %dynamic_update_slice.12 = f32[4,512,2,128]{1,0,3,2:T(4,128)} dynamic-update-slice(f32[4,512,2,128]{1,0,3,2:T(4,128)} %get-tuple-element.758, f32[1,512,2,128]{1,0,3,2:T(1,128)S(1)} %copy.278, s32[]{:T(128)S(6)} %copy.291, s32[]{:T(128)} %constant.104.clone.1..sunk.1, s32[]{:T(128)} %constant.104.clone.1..sunk.1, s32[]{:T(128)} %constant.104.clone.1..sunk.1) | dynamic-update-slice | bytes 1048580 | tf_op jit(solution)/shard_map/while/body/jit(dynamic_update_index_in_dim)/dynamic_update_slice | solution.py:190
  125.0 3.0 fusion.150
  130.7 3.3 fusion.152
  141.6 11.1 %dynamic_update_slice.12 = f32[4,512,2,128]{1,0,3,2:T(4,128)} dynamic-update-slice(f32[4,512,2,128]{1,0,3,2:T(4,128)} %get-tuple-element.758, f32[1,512,2,128]{1,0,3,2:T(1,128)S(1)} %copy.278, s32[]{:T(128)S(6)} %copy.291, s32[]{:T(128)} %constant.104.clone.1..sunk.1, s32[]{:T(128)} %constant.104.clone.1..sunk.1, s32[]{:T(128)} %constant.104.clone.1..sunk.1) | dynamic-update-slice | bytes 1048580 | tf_op jit(solution)/shard_map/while/body/jit(dynamic_update_index_in_dim)/dynamic_update_slice | solution.py:190
  153.4 3.0 reshape.322
  163.5 3.7 copy.206
  167.2 3.7 copy.208
  172.1 64.1 %while.41 = (s32[]{:T(128)}, f32[2,1024,2,128]{1,0,3,2:T(2,128)}, bf16[2,1024,2,128]{3,1,2,0:T(8,128)(2,1)}, bf16[16,2,128]{2,0,1:T(8,128)(2,1)S(1)}, s32[2,1024...) while((s32[]{:T(128)}, f32[2,1024,2,128]{1,0,3,2:T(2,128)}, ...), condition=%wide.region_6.7_spmd, body=%wide.region_1.6_spmd.sunk | while | flops 1119318016 | bytes 39351420 | solution.py:231
  173.5 3.0 fusion.138
  179.9 4.3 fusion.142
  185.4 18.9 %dynamic_update_slice.11 = f32[2,1024,2,128]{1,0,3,2:T(2,128)} dynamic-update-slice(f32[2,1024,2,128]{1,0,3,2:T(2,128)} %get-tuple-element.723, f32[1,1024,2,128]{1,0,3,2:T(1,128)S(1)} %copy.275, s32[]{:T(128)S(6)} %copy.283, s32[]{:T(128)} %constant.104.clone.1..sunk, s32[]{:T(128)} %constant.104.clone.1..sunk, s32[]{:T(128)} %constant.104.clone.1..sunk) | dynamic-update-slice | bytes 2097156 | tf_op jit(solution)/shard_map/while/body/jit(dynamic_update_index_in_dim)/dynamic_update_slice | solution.py:231
  205.6 3.0 fusion.138
  212.0 4.3 fusion.142
  217.5 18.8 %dynamic_update_slice.11 = f32[2,1024,2,128]{1,0,3,2:T(2,128)} dynamic-update-slice(f32[2,1024,2,128]{1,0,3,2:T(2,128)} %get-tuple-element.723, f32[1,1024,2,128]{1,0,3,2:T(1,128)S(1)} %copy.275, s32[]{:T(128)S(6)} %copy.283, s32[]{:T(128)} %constant.104.clone.1..sunk, s32[]{:T(128)} %constant.104.clone.1..sunk, s32[]{:T(128)} %constant.104.clone.1..sunk) | dynamic-update-slice | bytes 2097156 | tf_op jit(solution)/shard_map/while/body/jit(dynamic_update_index_in_dim)/dynamic_update_slice | solution.py:231
  236.3 4.0 reshape.328
  258.4 26.0 %all-gather.1 = f32[32,1,2]{2,1,0:T(1,128)} all-gather(f32[1,1,2]{2,1,0:T(1,128)S(1)} %bitcast.265), channel_id=1, replica_groups=mesh['req'=32,'tp'=4] {'req'}, dimensions={0}, use_global_device_ids=true | all-gather | bytes 264 | tf_op jit(solution)/shard_map/all_gather | solution.py:18
  289.4 62.7 %all-reduce.2 = (f32[32]{0:T(128)}, f32[32]{0:T(128)}) all-reduce(f32[32]{0:T(128)} %convert_dynamic-update-slice_fusion.1, f32[32]{0:T(128)} %convert_dynamic-update-slice_fusion), channel_id=1, replica_groups=mesh['req'=32,'tp'=4] {'req'}, use_global_device_ids=true, to_apply=%add | all-reduce | flops 64 | bytes 512
  352.1 255.1 %while.43 = (s32[]{:T(128)}, f32[2,128,128]{2,1,0:T(8,128)}, f32[]{:T(128)}, s32[]{:T(128)}, f32[32,2]{1,0:T(8,128)}, /*index=5*/f32[32]{0:T(128)}, f32[32,2,128...) while((s32[]{:T(128)}, f32[2,128,128]{2,1,0:T(8,128)}, ...), condition=%wide.region_16.17_spmd.clone, body=%wide.region_15.16_spmd.clone.sunk | while | flops 131087 | bytes 393486 | solution.py:30
  608.8 4.3 multiply_reduce_fusion
  614.2 4.5 fusion.98
  620.8 6.2 all-to-all-start
  628.3 3.7 copy.224
  632.0 3.7 copy.223
  635.8 5.7 pad_maximum_fusion
  644.1 5.0 fusion.61
  649.6 6.8 reduce.10
  656.4 6.6 reshape.365
  663.0 114.6 %all-reduce.6.cloned.1.call-done = f32[2048,1024]{1,0:T(8,128)} async-done(((f32[2048,1024]{1,0:T(8,128)}), f32[2048,1024]{1,0:T(8,128)}) %all-reduce.6.cloned.1.call-update) | async-done | bytes 8388624 | tf_op jit(solution)/shard_map/psum | solution.py:241
  777.6 5.9 fusion.66
  785.5 5.1 fusion.78
  790.6 7.9 all-to-all-start.1
  798.7 10.8 %convolution_convert_fusion.2 = bf16[2048,1024]{1,0:T(8,128)(2,1)} fusion(bf16[704,1024]{1,0:T(8,128)(2,1)S(1)} %copy-done, f32[2048,704]{0,1:T(8,128)} %fusion.78, bf16[1024,704]{0,1:T(8,128)(2,1)S(1)} %copy-done.24, bf16[2048,1024]{1,0:T(8,128)(2,1)} %copy-done.1, f32[1024]{0:T(1024)S(1)} %copy-done.20, f32[2048]{0:T(1024)S(1)} %add_rsqrt_fusion.3), kind=kOutput, calls=%fused_computation.108 | convolution fusion | flops 5924716544 | bytes 17051648 | tf_op jit(solution)/shard_map/dot_general | solution.py:248
  809.9 40.8 %all-to-all-done.1 = bf16[32,2,32768]{2,1,0:T(2,128)(2,1)} async-done(((bf16[32,2,32768]{2,1,0:T(2,128)(2,1)}), bf16[32,2,32768]{2,1,0:T(2,128)(2,1)}, u32[]{:S(2)}, u32[]{:S(2)}) %all-to-all-start.1) | async-done | bytes 4194336 | tf_op jit(solution)/shard_map/all_to_all | solution.py:137
  850.7 19.8 %reshape.366 = bf16[32,1,65536]{2,1,0:T(2,128)(2,1)} reshape(bf16[32,2,32768]{2,1,0:T(2,128)(2,1)} %all-to-all-done.1) | data formatting | bytes 8388608
  870.6 8.0 convolution_convert_fusion.1
  880.6 21.5 %all-reduce.8.cloned.1.call-done = bf16[2048,1024]{1,0:T(8,128)(2,1)} async-done(((bf16[2048,1024]{1,0:T(8,128)(2,1)}), bf16[2048,1024]{1,0:T(8,128)(2,1)}) %all-reduce.8.cloned.1.call-update) | async-done | bytes 4194320 | tf_op jit(solution)/shard_map/psum | solution.py:247
  902.1 7.6 fusion.69
  (336 shorter events, 292.4 us)
Async XLA Ops:
  7.2 791.6 %copy-start = (bf16[704,1024]{1,0:T(8,128)(2,1)S(1)}, bf16[704,1024]{1,0:T(8,128)(2,1)}, u32[]{:S(2)}) copy-start(bf16[704,1024]{1,0:T(8,128)(2,1)} %param.36) | copy-start | bytes 4325380
  7.2 344.9 %all-gather.4.cloned.1.call-start = ((), (), s32[]{:S(2)}) async-start(), calls=%async_computation.4 | async-start | bytes 4325376 | tf_op jit(solution)/shard_map/all_gather | solution.py:18
  7.2 4.2 copy-start.2
  11.5 3.6 copy-start.25
  15.1 5.1 copy-start.5
  15.1 2.5 copy-start.26
  17.6 9.0 copy-start.3
  25.7 7.7 copy-start.7
  26.6 9.4 %copy-start.13 = (f32[2048,2]{0,1:T(2,128)}, f32[2048,2]{0,1:T(2,128)S(1)}, u32[]{:S(2)}) copy-start(f32[2048,2]{0,1:T(2,128)S(1)} %add_rsqrt_fusion.1) | copy-start | bytes 49156
  29.3 3.0 copy-start.17
  29.3 3.6 copy-start.16
  153.3 7.0 copy-start.8
  153.3 8.6 copy-start.6
  153.3 624.3 %all-reduce.6.cloned.1.call-start = ((), (), s32[]{:S(2)}) async-start(), calls=%async_computation.2 | async-start | bytes 16777216 | tf_op jit(solution)/shard_map/psum | solution.py:241
  161.9 9.0 copy-start.11
  163.5 8.7 copy-start.18
  163.5 8.7 copy-start.19
  243.0 365.9 %copy-start.14 = (f32[2048,2]{0,1:T(2,128)S(1)}, f32[2048,2]{0,1:T(2,128)}, u32[]{:S(2)}) copy-start(f32[2048,2]{0,1:T(2,128)} %copy-done.13) | copy-start | bytes 49156
  249.8 0.6 copy-start.15
  607.2 6.0 copy-start.10
  607.2 6.0 copy-start.21
  613.2 1.0 copy-start.12
  618.7 0.7 copy-start.27
  618.7 0.8 copy-start.28
  618.7 9.6 %copy-start.9 = (bf16[2048,256]{0,1:T(8,128)(2,1)S(1)}, bf16[2048,256]{0,1:T(8,128)(2,1)}, u32[]{:S(2)}) copy-start(bf16[2048,256]{0,1:T(8,128)(2,1)} %convolution_convert_fusion.3) | copy-start | bytes 3145732
  618.7 13.3 %copy-start.4 = (bf16[2048,256]{0,1:T(8,128)(2,1)S(1)}, bf16[2048,256]{0,1:T(8,128)(2,1)}, u32[]{:S(2)}) copy-start(bf16[2048,256]{0,1:T(8,128)(2,1)} %copy-done.3) | copy-start | bytes 3145732
  619.5 0.5 copy-start.22
  620.8 169.8 %all-to-all-start = ((bf16[32,1,1]{2,1,0:T(2,128)(2,1)}), bf16[32,1,1]{2,1,0:T(2,128)(2,1)S(1)}, u32[]{:S(2)}, u32[]{:S(2)}) async-start(bf16[32,1,1]{2,1,0:T(2,128)(2,1)} %copy.222), calls=%async_computation | async-start | bytes 32768 | tf_op jit(solution)/shard_map/all_to_all | solution.py:138
  663.0 122.5 %copy-start.20 = (f32[1024]{0:T(1024)S(1)}, f32[1024]{0:T(1024)}, u32[]{:S(2)}) copy-start(f32[1024]{0:T(1024)} %convert_element_type.185) | copy-start | bytes 12292
  663.0 122.5 %copy-start.23 = (bf16[1024,704]{0,1:T(8,128)(2,1)S(1)}, bf16[1024,704]{0,1:T(8,128)(2,1)}, u32[]{:S(2)}) copy-start(bf16[1024,704]{0,1:T(8,128)(2,1)} %param.34) | copy-start | bytes 4325380
  783.5 2.0 copy-start.1
  790.6 8.1 copy-start.24
  790.6 60.1 %all-to-all-start.1 = ((bf16[32,2,32768]{2,1,0:T(2,128)(2,1)}), bf16[32,2,32768]{2,1,0:T(2,128)(2,1)}, u32[]{:S(2)}, u32[]{:S(2)}) async-start(bf16[32,2,32768]{2,1,0:T(2,128)(2,1)} %reshape.365), calls=%async_computation.1 | async-start | bytes 8388608 | tf_op jit(solution)/shard_map/all_to_all | solution.py:137
  798.5 103.6 %all-reduce.8.cloned.1.call-start = ((), (), s32[]{:S(2)}) async-start(), calls=%async_computation.3 | async-start | bytes 8388608 | tf_op jit(solution)/shard_map/psum | solution.py:247
Sparse Core Ops, SparseCore 0:
  153.5 49.9 all-gather.3
  618.9 158.6 all-reduce.5
  809.7 92.3 all-reduce.7
where the time goes:
time: 932 us; the launch traced here: 916 us
  local copies, waits for them, and re-layouts  271 us (29%)
  waiting for transfers between devices  177 us (19%)
  other arithmetic  156 us (17%)
  matrix products  107 us (11%)
  blocking collectives  88.7 us (10%)
  loops' own time  86.5 us (9%)
  between operations  15.5 us (2%)
  starting transfers between devices  14.3 us (2%)
    psum x1, waiting for transfers between devices, on_device(): lax.psum(jnp.dot(heads_out, w_out, preferred_element_type=jnp.float32), '...  115 us
    another operation x1, loops' own time, entering(): return lax.fori_loop(0, devices, step, start)  81.6 us
    dynamic_slice x64, local copies, waits for them, and re-layouts, step(): new = combine(before, jax.tree.map(lambda part: part[k], everything))  79.4 us
    unnamed x1, blocking collectives  62.7 us
    select_n x32, other arithmetic, step(): return jax.tree.map(lambda a, b: jnp.where(reached, a, b), new, before)  54.3 us
    dynamic_update_slice x8, local copies, waits for them, and re-layouts, on_device(): lax.scan(memory_block, start, (q_unit.reshape(mem_shape), k_unit.reshape(...  46.6 us
    all_to_all x1, waiting for transfers between devices, place_pages(): lax.all_to_all(outgoing, 'req', split_axis=0, concat_axis=0, tiled=True)  40.8 us
    mul x32, other arithmetic, combine_maps(): carry_factor = later[0] * joins  39.9 us
  transfers between devices with their start and end apart: 5, of which 3 were waited for; matrix products, arithmetic and copies ran while one was open for 21% of the time, Pallas kernels for 0%

commit v1 on v0

--- a/solution.py
+++ b/solution.py
@@ -3,6 +3,7 @@
 import jax.numpy as jnp
 from jax import lax
 from jax.sharding import PartitionSpec as P
+from jax.lax import all_gather
 
 HEAD_DIM = 128
 PERSIST = 16
@@ -244,7 +245,8 @@
     gate_proj = jnp.dot(normed_ffn, w_gate, preferred_element_type=jnp.float32)
     up_proj = jnp.dot(normed_ffn, w_up, preferred_element_type=jnp.float32)
     hidden = (jax.nn.silu(gate_proj) * up_proj).astype(jnp.bfloat16)
-    unit_total = lax.psum(
+    choose_cubes = lambda vector, bus_axis: all_gather(vector, bus_axis).sum(axis=0)
+    unit_total = choose_cubes(
         jnp.dot(hidden, w_down, preferred_element_type=jnp.float32).astype(jnp.bfloat16), "tp"
     ).astype(jnp.float32)
     layer_out = (resid.astype(jnp.float32) + unit_total).astype(jnp.bfloat16)

time: 932 us -> 970 us (1.041)
  waiting for transfers between devices: 177 us -> 229 us
    psum x1, waiting for transfers between devices: 115 us -> 158 us  [on_device(): lax.psum(jnp.dot(heads_out, w_out, preferred_element_type=jnp.float32), '...]
    psum x1 -> x0, waiting for transfers between devices: 21.5 us -> none  [on_device(): lax.psum(jnp.dot(hidden, w_down, preferred_element_type=jnp.float32).asty...]
    all_gather x0 -> x1, waiting for transfers between devices: none -> 19.3 us  [on_device(): all_gather(vector, bus_axis).sum(axis=0)]
    mul x32, other arithmetic: 39.9 us -> 22.1 us  [combine_maps(): carry_factor = later[0] * joins]
    reduce_sum x0 -> x1, other arithmetic: none -> 12 us  [on_device(): all_gather(vector, bus_axis).sum(axis=0)]
    all_to_all x1, waiting for transfers between devices: 40.8 us -> 51.7 us  [place_pages(): lax.all_to_all(outgoing, 'req', split_axis=0, concat_axis=0, tiled=True)]
    unnamed x67 -> x59, local copies, waits for them, and re-layouts: 39 us -> 40.4 us
  transfers between devices with their start and end apart: 5 -> 5, of which waited for: 3 -> 3; matrix products, arithmetic and copies ran while one was open for 21% -> 18% of each run, Pallas kernels for 0% -> 0%
where the time goes in v1:
time: 970 us; the launch traced here: 954 us
  local copies, waits for them, and re-layouts  268 us (28%)
  waiting for transfers between devices  229 us (24%)
  other arithmetic  147 us (15%)
  matrix products  103 us (11%)
  blocking collectives  88.7 us (9%)
  loops' own time  85.9 us (9%)
  starting transfers between devices  16.2 us (2%)
  between operations  15.6 us (2%)
    psum x1, waiting for transfers between devices, on_device(): lax.psum(jnp.dot(heads_out, w_out, preferred_element_type=jnp.float32), '...  158 us
    dynamic_slice x64, local copies, waits for them, and re-layouts, step(): new = combine(before, jax.tree.map(lambda part: part[k], everything))  81.9 us
    another operation x1, loops' own time, entering(): return lax.fori_loop(0, devices, step, start)  80.2 us
    unnamed x1, blocking collectives  62.8 us
    select_n x32, other arithmetic, step(): return jax.tree.map(lambda a, b: jnp.where(reached, a, b), new, before)  54.2 us
    all_to_all x1, waiting for transfers between devices, place_pages(): lax.all_to_all(outgoing, 'req', split_axis=0, concat_axis=0, tiled=True)  51.7 us
    dynamic_update_slice x8, local copies, waits for them, and re-layouts, on_device(): lax.scan(memory_block, start, (q_unit.reshape(mem_shape), k_unit.reshape(...  46.5 us
    unnamed x59, local copies, waits for them, and re-layouts  40.4 us
  transfers between devices with their start and end apart: 5, of which 3 were waited for; matrix products, arithmetic and copies ran while one was open for 18% of the time, Pallas kernels for 0%

profile of v1, /device:TPU:1, one launch (start us, length us, event | category | flops | bytes accessed | tf_op | source)
XLA Modules:
  0.0 954.2 jit_solution(13572917156794966078)
XLA Ops:
  8.0 3.1 fusion.62
  11.1 3.8 convolution_convert_fusion.3
  19.2 4.0 bitcast_reduce_fusion
  26.0 3.7 reshape.341
  38.3 4.2 multiply_multiply_fusion
  42.5 100.3 %while.42 = (s32[]{:T(128)}, f32[2,128,128]{2,1,0:T(8,128)S(1)}, s32[]{:T(128)}, f32[4,512,2,128]{1,0,3,2:T(4,128)}, f32[4,512,2,128]{3,1,2,0:T(8,128)}, /*index...) while((s32[]{:T(128)}, f32[2,128,128]{2,1,0:T(8,128)S(1)}, ...), condition=%wide.region_12.13_spmd.clone, body=%wide.region_9.12_spmd.clone.sunk | while | flops 2016809984 | bytes 11492285 | solution.py:191
  46.2 3.0 fusion.150
  55.9 11.1 %dynamic_update_slice.12 = f32[4,512,2,128]{1,0,3,2:T(4,128)} dynamic-update-slice(f32[4,512,2,128]{1,0,3,2:T(4,128)} %get-tuple-element.758, f32[1,512,2,128]{1,0,3,2:T(1,128)S(1)} %copy.278, s32[]{:T(128)S(6)} %copy.291, s32[]{:T(128)} %constant.105.clone.1..sunk.1, s32[]{:T(128)} %constant.105.clone.1..sunk.1, s32[]{:T(128)} %constant.105.clone.1..sunk.1) | dynamic-update-slice | bytes 1048580 | tf_op jit(solution)/shard_map/while/body/jit(dynamic_update_index_in_dim)/dynamic_update_slice | solution.py:191
  71.2 3.0 fusion.150
  81.0 11.1 %dynamic_update_slice.12 = f32[4,512,2,128]{1,0,3,2:T(4,128)} dynamic-update-slice(f32[4,512,2,128]{1,0,3,2:T(4,128)} %get-tuple-element.758, f32[1,512,2,128]{1,0,3,2:T(1,128)S(1)} %copy.278, s32[]{:T(128)S(6)} %copy.291, s32[]{:T(128)} %constant.105.clone.1..sunk.1, s32[]{:T(128)} %constant.105.clone.1..sunk.1, s32[]{:T(128)} %constant.105.clone.1..sunk.1) | dynamic-update-slice | bytes 1048580 | tf_op jit(solution)/shard_map/while/body/jit(dynamic_update_index_in_dim)/dynamic_update_slice | solution.py:191
  96.3 3.0 fusion.150
  106.0 11.1 %dynamic_update_slice.12 = f32[4,512,2,128]{1,0,3,2:T(4,128)} dynamic-update-slice(f32[4,512,2,128]{1,0,3,2:T(4,128)} %get-tuple-element.758, f32[1,512,2,128]{1,0,3,2:T(1,128)S(1)} %copy.278, s32[]{:T(128)S(6)} %copy.291, s32[]{:T(128)} %constant.105.clone.1..sunk.1, s32[]{:T(128)} %constant.105.clone.1..sunk.1, s32[]{:T(128)} %constant.105.clone.1..sunk.1) | dynamic-update-slice | bytes 1048580 | tf_op jit(solution)/shard_map/while/body/jit(dynamic_update_index_in_dim)/dynamic_update_slice | solution.py:191
  121.3 3.0 fusion.150
  131.0 11.1 %dynamic_update_slice.12 = f32[4,512,2,128]{1,0,3,2:T(4,128)} dynamic-update-slice(f32[4,512,2,128]{1,0,3,2:T(4,128)} %get-tuple-element.758, f32[1,512,2,128]{1,0,3,2:T(1,128)S(1)} %copy.278, s32[]{:T(128)S(6)} %copy.291, s32[]{:T(128)} %constant.105.clone.1..sunk.1, s32[]{:T(128)} %constant.105.clone.1..sunk.1, s32[]{:T(128)} %constant.105.clone.1..sunk.1) | dynamic-update-slice | bytes 1048580 | tf_op jit(solution)/shard_map/while/body/jit(dynamic_update_index_in_dim)/dynamic_update_slice | solution.py:191
  163.7 3.7 copy.208
  167.4 3.7 copy.206
  172.9 3.7 reshape.332
  176.7 64.1 %while.41 = (s32[]{:T(128)}, f32[2,1024,2,128]{1,0,3,2:T(2,128)}, bf16[2,1024,2,128]{3,1,2,0:T(8,128)(2,1)}, bf16[16,2,128]{2,0,1:T(8,128)(2,1)S(1)}, s32[2,1024...) while((s32[]{:T(128)}, f32[2,1024,2,128]{1,0,3,2:T(2,128)}, ...), condition=%wide.region_6.7_spmd, body=%wide.region_1.6_spmd.sunk | while | flops 1119318016 | bytes 39351420 | solution.py:232
  179.3 3.0 fusion.138
  184.4 4.3 fusion.142
  189.9 18.8 %dynamic_update_slice.11 = f32[2,1024,2,128]{1,0,3,2:T(2,128)} dynamic-update-slice(f32[2,1024,2,128]{1,0,3,2:T(2,128)} %get-tuple-element.723, f32[1,1024,2,128]{1,0,3,2:T(1,128)S(1)} %copy.275, s32[]{:T(128)S(6)} %copy.283, s32[]{:T(128)} %constant.105.clone.1..sunk, s32[]{:T(128)} %constant.105.clone.1..sunk, s32[]{:T(128)} %constant.105.clone.1..sunk) | dynamic-update-slice | bytes 2097156 | tf_op jit(solution)/shard_map/while/body/jit(dynamic_update_index_in_dim)/dynamic_update_slice | solution.py:232
  211.3 3.0 fusion.138
  216.4 4.3 fusion.142
  221.9 18.8 %dynamic_update_slice.11 = f32[2,1024,2,128]{1,0,3,2:T(2,128)} dynamic-update-slice(f32[2,1024,2,128]{1,0,3,2:T(2,128)} %get-tuple-element.723, f32[1,1024,2,128]{1,0,3,2:T(1,128)S(1)} %copy.275, s32[]{:T(128)S(6)} %copy.283, s32[]{:T(128)} %constant.105.clone.1..sunk, s32[]{:T(128)} %constant.105.clone.1..sunk, s32[]{:T(128)} %constant.105.clone.1..sunk) | dynamic-update-slice | bytes 2097156 | tf_op jit(solution)/shard_map/while/body/jit(dynamic_update_index_in_dim)/dynamic_update_slice | solution.py:232
  240.7 4.2 reshape.328
  247.0 25.8 %all-gather.2 = f32[32,1,2]{2,1,0:T(1,128)} all-gather(f32[1,1,2]{2,1,0:T(1,128)S(1)} %bitcast.267), channel_id=1, replica_groups=mesh['req'=32,'tp'=4] {'req'}, dimensions={0}, use_global_device_ids=true | all-gather | bytes 264 | tf_op jit(solution)/shard_map/all_gather | solution.py:19
  277.9 62.8 %all-reduce.2 = (f32[32]{0:T(128)}, f32[32]{0:T(128)}) all-reduce(f32[32]{0:T(128)} %convert_dynamic-update-slice_fusion.1, f32[32]{0:T(128)} %convert_dynamic-update-slice_fusion), channel_id=1, replica_groups=mesh['req'=32,'tp'=4] {'req'}, use_global_device_ids=true, to_apply=%add | all-reduce | flops 64 | bytes 512
  340.8 238.4 %while.43 = (s32[]{:T(128)}, f32[2,128,128]{2,1,0:T(8,128)}, f32[]{:T(128)}, s32[]{:T(128)}, f32[32,2]{1,0:T(8,128)}, /*index=5*/f32[32]{0:T(128)}, f32[32,2,128...) while((s32[]{:T(128)}, f32[2,128,128]{2,1,0:T(8,128)}, ...), condition=%wide.region_16.17_spmd.clone, body=%wide.region_15.16_spmd.clone.sunk | while | flops 131087 | bytes 393486 | solution.py:31
  580.8 4.3 multiply_reduce_fusion
  586.1 4.5 fusion.98
  591.3 158.3 %all-reduce.5.cloned.1.call-done = f32[2048,1024]{1,0:T(8,128)} async-done(((f32[2048,1024]{1,0:T(8,128)}), f32[2048,1024]{1,0:T(8,128)}) %all-reduce.5.cloned.1.call-update) | async-done | bytes 8388624 | tf_op jit(solution)/shard_map/psum | solution.py:242
  749.6 5.9 fusion.66
  757.4 5.1 fusion.78
  762.6 11.2 %convolution_convert_fusion.2 = bf16[2048,1024]{1,0:T(8,128)(2,1)} fusion(bf16[704,1024]{1,0:T(8,128)(2,1)S(1)} %copy-done, f32[2048,704]{0,1:T(8,128)} %fusion.78, bf16[1024,704]{0,1:T(8,128)(2,1)} %param.35, bf16[2048,1024]{1,0:T(8,128)(2,1)} %copy-done.1, f32[1024]{0:T(1024)S(1)} %convert_element_type.187, f32[2048]{0:T(1024)S(1)} %add_rsqrt_fusion.3), kind=kOutput, calls=%fused_computation.108 | convolution fusion | flops 5924716544 | bytes 17051648 | tf_op jit(solution)/shard_map/dot_general | solution.py:250
  775.9 8.2 all-to-all-start
  784.1 3.8 copy.223
  787.9 3.7 copy.224
  791.7 5.9 pad_maximum_fusion
  800.2 4.9 fusion.61
  805.5 6.9 reduce.11
  812.4 6.6 reshape.366
  819.0 7.8 all-to-all-start.1
  827.1 51.7 %all-to-all-done.1 = bf16[32,2,32768]{2,1,0:T(2,128)(2,1)} async-done(((bf16[32,2,32768]{2,1,0:T(2,128)(2,1)}), bf16[32,2,32768]{2,1,0:T(2,128)(2,1)}, u32[]{:S(2)}, u32[]{:S(2)}) %all-to-all-start.1) | async-done | bytes 4194336 | tf_op jit(solution)/shard_map/all_to_all | solution.py:138
  878.8 19.8 %reshape.367 = bf16[32,1,65536]{2,1,0:T(2,128)(2,1)} reshape(bf16[32,2,32768]{2,1,0:T(2,128)(2,1)} %all-to-all-done.1) | data formatting | bytes 8388608
  898.6 7.9 convolution_convert_fusion.1
  908.6 19.3 %all-gather.8.cloned.1.call-done = bf16[8192,1024]{1,0:T(8,128)(2,1)} async-done(((bf16[2048,1024]{1,0:T(8,128)(2,1)}), bf16[8192,1024]{1,0:T(8,128)(2,1)}) %all-gather.8.cloned.1.call-update) | async-done | bytes 16777232 | tf_op jit(solution)/shard_map/all_gather | solution.py:248
  927.9 12.0 %reduce_sum.98 = bf16[2048,1024]{1,0:T(8,128)(2,1)} reduce(bf16[4,2048,1024]{2,1,0:T(8,128)(2,1)} %bitcast.245, bf16[]{:T(256)} %constant.117.clone.1), dimensions={0}, to_apply=%region_20.21 | reduce | flops 6291456 | bytes 20971522 | tf_op jit(solution)/shard_map/reduce_sum | solution.py:248
  939.9 7.6 fusion.69
  (329 shorter events, 265.9 us)
Async XLA Ops:
  7.2 755.4 %copy-start = (bf16[704,1024]{1,0:T(8,128)(2,1)S(1)}, bf16[704,1024]{1,0:T(8,128)(2,1)}, u32[]{:S(2)}) copy-start(bf16[704,1024]{1,0:T(8,128)(2,1)} %param.36) | copy-start | bytes 4325380
  7.2 4.0 copy-start.15
  7.2 333.6 %all-gather.6.cloned.1.call-start = ((), (), s32[]{:S(2)}) async-start(), calls=%async_computation.3 | async-start | bytes 4325376 | tf_op jit(solution)/shard_map/all_gather | solution.py:19
  14.9 1.6 copy-start.6
  19.2 4.1 copy-start.2
  19.2 4.1 copy-start.22
  23.2 123.7 %copy-start.4 = (bf16[2048,256]{0,1:T(8,128)(2,1)}, bf16[2048,256]{0,1:T(8,128)(2,1)S(1)}, u32[]{:S(2)}) copy-start(bf16[2048,256]{0,1:T(8,128)(2,1)S(1)} %get-tuple-element.534) | copy-start | bytes 3145732
  26.0 12.3 %copy-start.11 = (f32[2048,2]{0,1:T(2,128)}, f32[2048,2]{0,1:T(2,128)S(1)}, u32[]{:S(2)}) copy-start(f32[2048,2]{0,1:T(2,128)S(1)} %add_rsqrt_fusion.1) | copy-start | bytes 49156
  38.3 4.2 copy-start.14
  142.8 0.7 copy-start.3
  143.4 606.1 %all-reduce.5.cloned.1.call-start = ((), (), s32[]{:S(2)}) async-start(), calls=%async_computation.2 | async-start | bytes 16777216 | tf_op jit(solution)/shard_map/psum | solution.py:242
  160.0 0.6 copy-start.13
  172.9 3.7 copy-start.16
  172.9 3.7 copy-start.17
  240.7 340.0 %copy-start.8 = (f32[2048,2,128]{2,0,1:T(8,128)S(1)}, f32[2048,2,128]{2,0,1:T(8,128)}, u32[]{:S(2)}) copy-start(f32[2048,2,128]{2,0,1:T(8,128)} %copy.220) | copy-start | bytes 6291460
  240.7 340.0 %copy-start.12 = (f32[2048,2]{0,1:T(2,128)S(1)}, f32[2048,2]{0,1:T(2,128)}, u32[]{:S(2)}) copy-start(f32[2048,2]{0,1:T(2,128)} %copy-done.11) | copy-start | bytes 49156
  579.2 6.0 copy-start.9
  579.2 6.0 copy-start.19
  585.1 1.0 copy-start.10
  590.6 0.7 copy-start.18
  590.6 337.3 %all-gather.8.cloned.1.call-start = ((), (), s32[]{:S(2)}) async-start(), calls=%async_computation.4 | async-start | bytes 20971520 | tf_op jit(solution)/shard_map/all_gather | solution.py:248
  591.3 166.1 %copy-start.21 = (bf16[1024,704]{0,1:T(8,128)(2,1)S(1)}, bf16[1024,704]{0,1:T(8,128)(2,1)}, u32[]{:S(2)}) copy-start(bf16[1024,704]{0,1:T(8,128)(2,1)} %param.34) | copy-start | bytes 4325380
  755.4 2.0 copy-start.1
  773.8 0.7 copy-start.23
  773.8 0.8 copy-start.24
  773.8 10.4 %copy-start.5 = (bf16[2048,256]{0,1:T(8,128)(2,1)S(1)}, bf16[2048,256]{0,1:T(8,128)(2,1)}, u32[]{:S(2)}) copy-start(bf16[2048,256]{0,1:T(8,128)(2,1)} %copy-done.4) | copy-start | bytes 3145732
  773.8 14.1 %copy-start.7 = (bf16[2048,256]{0,1:T(8,128)(2,1)S(1)}, bf16[2048,256]{0,1:T(8,128)(2,1)}, u32[]{:S(2)}) copy-start(bf16[2048,256]{0,1:T(8,128)(2,1)} %copy-done.6) | copy-start | bytes 3145732
  774.5 0.5 copy-start.20
  775.9 43.1 %all-to-all-start = ((bf16[32,1,1]{2,1,0:T(2,128)(2,1)}), bf16[32,1,1]{2,1,0:T(2,128)(2,1)S(1)}, u32[]{:S(2)}, u32[]{:S(2)}) async-start(bf16[32,1,1]{2,1,0:T(2,128)(2,1)} %copy.222), calls=%async_computation | async-start | bytes 32768 | tf_op jit(solution)/shard_map/all_to_all | solution.py:139
  819.0 59.8 %all-to-all-start.1 = ((bf16[32,2,32768]{2,1,0:T(2,128)(2,1)}), bf16[32,2,32768]{2,1,0:T(2,128)(2,1)}, u32[]{:S(2)}, u32[]{:S(2)}) async-start(bf16[32,2,32768]{2,1,0:T(2,128)(2,1)} %reshape.366), calls=%async_computation.1 | async-start | bytes 8388608 | tf_op jit(solution)/shard_map/all_to_all | solution.py:138
Sparse Core Ops, SparseCore 0:
  143.6 50.0 all-gather.5
  590.8 158.7 all-reduce.4
  773.9 153.9 all-gather.7
